TPU v7x, 32 devices: a whole 2x2x4 slice. The times are simulated.
32 devices in a mesh: fsdp: 32 (over z, y, x, core).
Axes of the slice: x: 2, y: 2, z: 4, core: 2. Of those that a mesh axis runs over, the one named last changes fastest.
Arguments:
- inputs: bfloat16 [6144, 1280], P('fsdp'), may hold values from -6 to 6
- ln1_gain: float32 [1280], P('fsdp'), may hold values from 0.5 to 1.5
- ln1_bias: float32 [1280], P('fsdp'), may hold values from -1 to 1
- w_query: float32 [1280, 1280], P('fsdp'), may hold values from -0.3125 to 0.3125
- b_query: float32 [1280], P('fsdp'), may hold values from -2.5 to 2.5
- w_key: float32 [1280, 1280], P('fsdp'), may hold values from -0.15625 to 0.15625
- w_value: float32 [1280, 1280], P('fsdp'), may hold values from -0.15625 to 0.15625
- b_value: float32 [1280], P('fsdp'), may hold values from -2.5 to 2.5
- w_out: float32 [1280, 1280], P('fsdp'), may hold values from -0.625 to 0.625
- b_out: float32 [1280], P('fsdp'), may hold values from -2.5 to 2.5
- ln2_gain: float32 [1280], P('fsdp'), may hold values from 0.5 to 1.5
- ln2_bias: float32 [1280], P('fsdp'), may hold values from -1 to 1
- w_up: float32 [1280, 5120], P('fsdp'), may hold values from -0.15625 to 0.15625
- b_up: float32 [5120], P('fsdp'), may hold values from -2.5 to 2.5
- w_down: float32 [5120, 1280], P('fsdp'), may hold values from -0.078125 to 0.078125
- b_down: float32 [1280], P('fsdp'), may hold values from -2.5 to 2.5
- lengths: int32 [4], replicated, may hold values from 1153 to 1536, as said below
- cotangent: bfloat16 [6144, 1280], P('fsdp'), may hold values from -6 to 6
Outputs:
- output: float32 [6144, 1280], P('fsdp')
- grad_inputs: float32 [6144, 1280], P('fsdp')
- grad_ln1_gain: float32 [1280], P('fsdp')
- grad_ln1_bias: float32 [1280], P('fsdp')
- grad_w_query: float32 [1280, 1280], P('fsdp')
- grad_b_query: float32 [1280], P('fsdp')
- grad_w_key: float32 [1280, 1280], P('fsdp')
- grad_w_value: float32 [1280, 1280], P('fsdp')
- grad_b_value: float32 [1280], P('fsdp')
- grad_w_out: float32 [1280, 1280], P('fsdp')
- grad_b_out: float32 [1280], P('fsdp')
- grad_ln2_gain: float32 [1280], P('fsdp')
- grad_ln2_bias: float32 [1280], P('fsdp')
- grad_w_up: float32 [1280, 5120], P('fsdp')
- grad_b_up: float32 [5120], P('fsdp')
- grad_w_down: float32 [5120, 1280], P('fsdp')
- grad_b_down: float32 [1280], P('fsdp')
Inputs may be any that keep to these rules, and one draw needn't show every extreme that they name: Frames of clip c at positions lengths[c] and beyond are padding; some clip has exactly 1536 real frames and some exactly 1153.
All inputs are finite; a program needn't handle non-finite values.
Results may differ from a plain program's by a relative error of at most 0.014.
The roundings to bfloat16 on the way count: a program that leaves them out, or rounds other values in their place, can miss the bound.
Values may be sent and summed in bfloat16 or wider, within the bound.
A program may use at most 320 MiB of HBM per device.

v0:
```python
import math
import jax
import jax.numpy as jnp
from jax import lax
from jax.sharding import PartitionSpec as P

D = 1280
H = 16
HD = 80
CLIP_LEN = 1536
epsilon = 1e-05
masked_value = -1e30


def swapped(block, axis, bit):
    count = lax.axis_size(axis)
    route = []
    for low in range(count):
        high = low | 1 << bit
        if high != low and high < count:
            route += [(low, high), (high, low)]
    return lax.ppermute(block, axis, route)


def layer_norm(values, gain, offset):
    average = jnp.mean(values, axis=-1, keepdims=True)
    centred = values - average
    variance = jnp.mean(centred * centred, axis=-1, keepdims=True)
    return centred * lax.rsqrt(variance + epsilon) * gain + offset


def norm_backward(values, gain, grad_out):

    def normalize(values_in, gain_in):
        return layer_norm(values_in, gain_in, 0.0)

    unused, pullback = jax.vjp(normalize, values, gain)
    grad_values, grad_gain = pullback(grad_out)
    return (grad_values, grad_gain, jnp.sum(grad_out, axis=0))


def gelu_exact(values):
    return jax.nn.gelu(values, approximate=False)


def matmul(left, right):
    return jnp.dot(left, right, preferred_element_type=jnp.float32)


def outer_sum(left, right):
    return lax.dot_general(
        left, right, (((0,), (0,)), ((), ())), preferred_element_type=jnp.float32
    )


def times_transposed(left, right):
    return lax.dot_general(
        left, right, (((1,), (1,)), ((), ())), preferred_element_type=jnp.float32
    )


def column_sums(matrix):
    return jnp.sum(matrix.astype(jnp.float32), axis=0)


def split_heads(matrix):
    return matrix.reshape(matrix.shape[0], H, HD).transpose(1, 0, 2)


def merge_heads(stacked):
    return stacked.transpose(1, 0, 2).reshape(stacked.shape[1], H * HD)


def on_device(
    inputs,
    ln1_gain,
    ln1_bias,
    w_query,
    b_query,
    w_key,
    w_value,
    b_value,
    w_out,
    b_out,
    ln2_gain,
    ln2_bias,
    w_up,
    b_up,
    w_down,
    b_down,
    lengths,
    cotangent,
):
    (
        whole_ln1_gain,
        whole_ln1_bias,
        whole_w_query,
        whole_b_query,
        whole_w_key,
        whole_w_value,
        whole_b_value,
        whole_w_out,
        whole_b_out,
        whole_ln2_gain,
        whole_ln2_bias,
        whole_w_up,
        whole_b_up,
        whole_w_down,
        whole_b_down,
    ) = (
        lax.all_gather(ln1_gain.astype(jnp.bfloat16), "fsdp", axis=0, tiled=True),
        lax.all_gather(ln1_bias.astype(jnp.bfloat16), "fsdp", axis=0, tiled=True),
        lax.all_gather(w_query.astype(jnp.bfloat16), "fsdp", axis=0, tiled=True),
        lax.all_gather(b_query.astype(jnp.bfloat16), "fsdp", axis=0, tiled=True),
        lax.all_gather(w_key.astype(jnp.bfloat16), "fsdp", axis=0, tiled=True),
        lax.all_gather(w_value.astype(jnp.bfloat16), "fsdp", axis=0, tiled=True),
        lax.all_gather(b_value.astype(jnp.bfloat16), "fsdp", axis=0, tiled=True),
        lax.all_gather(w_out.astype(jnp.bfloat16), "fsdp", axis=0, tiled=True),
        lax.all_gather(b_out.astype(jnp.bfloat16), "fsdp", axis=0, tiled=True),
        lax.all_gather(ln2_gain.astype(jnp.bfloat16), "fsdp", axis=0, tiled=True),
        lax.all_gather(ln2_bias.astype(jnp.bfloat16), "fsdp", axis=0, tiled=True),
        lax.all_gather(w_up.astype(jnp.bfloat16), "fsdp", axis=0, tiled=True),
        lax.all_gather(b_up.astype(jnp.bfloat16), "fsdp", axis=0, tiled=True),
        lax.all_gather(w_down.astype(jnp.bfloat16), "fsdp", axis=0, tiled=True),
        lax.all_gather(b_down.astype(jnp.bfloat16), "fsdp", axis=0, tiled=True),
    )
    device_index = lax.axis_index("fsdp")
    row_count = inputs.shape[0]
    group_size = CLIP_LEN // row_count
    levels = group_size.bit_length() - 1
    length = lengths[device_index // group_size]
    key_valid = (jnp.arange(CLIP_LEN, dtype=jnp.int32) < length)[None, :]
    score_scale = 1.0 / math.sqrt(HD)
    source = inputs.astype(jnp.float32)
    normed = layer_norm(
        source, whole_ln1_gain.astype(jnp.float32), whole_ln1_bias.astype(jnp.float32)
    ).astype(jnp.bfloat16)
    query_rows = (matmul(normed, whole_w_query) + whole_b_query.astype(jnp.float32)).astype(
        jnp.bfloat16
    )
    key_rows = matmul(normed, whole_w_key).astype(jnp.bfloat16)
    value_rows = (matmul(normed, whole_w_value) + whole_b_value.astype(jnp.float32)).astype(
        jnp.bfloat16
    )
    key_all, value_all = (key_rows, value_rows)
    for bit_number in range(levels):
        other_key, other_value = swapped((key_all, value_all), "fsdp", bit_number)
        upper_half = device_index // (1 << bit_number) % 2 == 1
        key_all = jnp.where(
            upper_half,
            jnp.concatenate([other_key, key_all], axis=0),
            jnp.concatenate([key_all, other_key], axis=0),
        )
        value_all = jnp.where(
            upper_half,
            jnp.concatenate([other_value, value_all], axis=0),
            jnp.concatenate([value_all, other_value], axis=0),
        )

    def head_scores(query_head, key_head):
        scores = times_transposed(query_head, key_head) * score_scale
        return jnp.where(key_valid, scores, masked_value)

    def head_forward(operands):
        query_head, key_head, value_head = operands
        masked = head_scores(query_head, key_head)
        largest = jnp.max(masked, axis=-1, keepdims=True)
        exponent = jnp.exp(masked - largest)
        total = jnp.sum(exponent, axis=-1, keepdims=True)
        attn_weights = (exponent / total).astype(jnp.bfloat16)
        return (matmul(attn_weights, value_head), (largest + jnp.log(total))[:, 0])

    query_heads = split_heads(query_rows)
    key_heads = split_heads(key_all)
    value_heads = split_heads(value_all)
    mixed_heads, log_totals = lax.map(head_forward, (query_heads, key_heads, value_heads))
    attended = merge_heads(mixed_heads).astype(jnp.bfloat16)
    residual = source + (matmul(attended, whole_w_out) + whole_b_out.astype(jnp.float32))
    normed_two = layer_norm(
        residual, whole_ln2_gain.astype(jnp.float32), whole_ln2_bias.astype(jnp.float32)
    ).astype(jnp.bfloat16)
    hidden = matmul(normed_two, whole_w_up) + whole_b_up.astype(jnp.float32)
    activated = gelu_exact(hidden).astype(jnp.bfloat16)
    output = residual + (matmul(activated, whole_w_down) + whole_b_down.astype(jnp.float32))
    (
        back_w_query,
        back_w_key,
        back_w_value,
        back_w_out,
        back_w_up,
        back_w_down,
        back_ln1_gain,
        back_ln2_gain,
    ) = (
        lax.all_gather(w_query.astype(jnp.bfloat16), "fsdp", axis=0, tiled=True),
        lax.all_gather(w_key.astype(jnp.bfloat16), "fsdp", axis=0, tiled=True),
        lax.all_gather(w_value.astype(jnp.bfloat16), "fsdp", axis=0, tiled=True),
        lax.all_gather(w_out.astype(jnp.bfloat16), "fsdp", axis=0, tiled=True),
        lax.all_gather(w_up.astype(jnp.bfloat16), "fsdp", axis=0, tiled=True),
        lax.all_gather(w_down.astype(jnp.bfloat16), "fsdp", axis=0, tiled=True),
        lax.all_gather(ln1_gain.astype(jnp.bfloat16), "fsdp", axis=0, tiled=True),
        lax.all_gather(ln2_gain.astype(jnp.bfloat16), "fsdp", axis=0, tiled=True),
    )
    grad_b_down = column_sums(cotangent)
    grad_activated = times_transposed(cotangent, back_w_down)
    unused, gelu_pullback = jax.vjp(gelu_exact, hidden)
    grad_hidden = gelu_pullback(grad_activated)[0].astype(jnp.bfloat16)
    shard_w_down = lax.psum_scatter(
        outer_sum(activated, cotangent), "fsdp", scatter_dimension=0, tiled=True
    )
    grad_b_up = column_sums(grad_hidden)
    grad_normed_two = times_transposed(grad_hidden, back_w_up)
    grad_from_second, grad_ln2_gain, grad_ln2_bias = norm_backward(
        residual, back_ln2_gain.astype(jnp.float32), grad_normed_two
    )
    grad_residual = cotangent.astype(jnp.float32) + grad_from_second
    grad_branch = grad_residual.astype(jnp.bfloat16)
    grad_b_out = column_sums(grad_branch)
    grad_attended = times_transposed(grad_branch, back_w_out).astype(jnp.bfloat16)

    def head_backward(operands):
        query_head, key_head, value_head, grad_head, log_total = operands
        masked = head_scores(query_head, key_head)
        attn_weights = jnp.exp(masked - log_total[:, None])
        grad_weights = times_transposed(grad_head, value_head)
        inner = jnp.sum(attn_weights * grad_weights, axis=-1, keepdims=True)
        grad_scores = (attn_weights * (grad_weights - inner)).astype(jnp.bfloat16)
        grad_query = matmul(grad_scores, key_head) * score_scale
        grad_key = outer_sum(grad_scores, query_head) * score_scale
        grad_value = outer_sum(attn_weights.astype(jnp.bfloat16), grad_head)
        return (grad_query, grad_key, grad_value)

    grad_query_heads, grad_key_heads, grad_value_heads = lax.map(
        head_backward, (query_heads, key_heads, value_heads, split_heads(grad_attended), log_totals)
    )
    grad_queries = merge_heads(grad_query_heads).astype(jnp.bfloat16)
    grad_key_all = merge_heads(grad_key_heads)
    grad_value_all = merge_heads(grad_value_heads)
    for bit_number in reversed(range(levels)):
        half_rows = grad_key_all.shape[0] // 2
        upper_half = device_index // (1 << bit_number) % 2 == 1
        lower_key, higher_key = (grad_key_all[:half_rows], grad_key_all[half_rows:])
        lower_value, higher_value = (grad_value_all[:half_rows], grad_value_all[half_rows:])
        keep_key = jnp.where(upper_half, higher_key, lower_key)
        send_key = jnp.where(upper_half, lower_key, higher_key)
        keep_value = jnp.where(upper_half, higher_value, lower_value)
        send_value = jnp.where(upper_half, lower_value, higher_value)
        got_key, got_value = (
            swapped(send_key.astype(jnp.bfloat16), "fsdp", bit_number).astype(send_key.dtype),
            swapped(send_value.astype(jnp.bfloat16), "fsdp", bit_number).astype(send_value.dtype),
        )
        grad_key_all = keep_key + got_key
        grad_value_all = keep_value + got_value
    grad_keys = grad_key_all.astype(jnp.bfloat16)
    grad_values = grad_value_all.astype(jnp.bfloat16)
    grad_b_query = column_sums(grad_queries)
    grad_b_value = column_sums(grad_values)
    grad_normed = (
        times_transposed(grad_queries, back_w_query)
        + times_transposed(grad_keys, back_w_key)
        + times_transposed(grad_values, back_w_value)
    )
    grad_from_first, grad_ln1_gain, grad_ln1_bias = norm_backward(
        source, back_ln1_gain.astype(jnp.float32), grad_normed
    )
    grad_inputs = grad_residual + grad_from_first
    stacked = lax.psum_scatter(
        jnp.concatenate(
            [
                jnp.concatenate(
                    [
                        outer_sum(normed, grad_queries),
                        outer_sum(normed, grad_keys),
                        outer_sum(normed, grad_values),
                        outer_sum(attended, grad_branch),
                    ],
                    axis=1,
                ),
                outer_sum(normed_two, grad_hidden),
            ],
            axis=1,
        ),
        "fsdp",
        scatter_dimension=0,
        tiled=True,
    )
    shard_w_up = stacked[:, 4 * D :]
    shard_w_query = stacked[:, 0:D]
    shard_w_key = stacked[:, D : 2 * D]
    shard_w_value = stacked[:, 2 * D : 3 * D]
    shard_w_out = stacked[:, 3 * D : 4 * D]
    (
        shard_ln1_gain,
        shard_ln1_bias,
        shard_b_query,
        shard_b_value,
        shard_b_out,
        shard_ln2_gain,
        shard_ln2_bias,
        shard_b_up,
        shard_b_down,
    ) = (
        lax.psum_scatter(grad_ln1_gain, "fsdp", scatter_dimension=0, tiled=True),
        lax.psum_scatter(grad_ln1_bias, "fsdp", scatter_dimension=0, tiled=True),
        lax.psum_scatter(grad_b_query, "fsdp", scatter_dimension=0, tiled=True),
        lax.psum_scatter(grad_b_value, "fsdp", scatter_dimension=0, tiled=True),
        lax.psum_scatter(grad_b_out, "fsdp", scatter_dimension=0, tiled=True),
        lax.psum_scatter(grad_ln2_gain, "fsdp", scatter_dimension=0, tiled=True),
        lax.psum_scatter(grad_ln2_bias, "fsdp", scatter_dimension=0, tiled=True),
        lax.psum_scatter(grad_b_up, "fsdp", scatter_dimension=0, tiled=True),
        lax.psum_scatter(grad_b_down, "fsdp", scatter_dimension=0, tiled=True),
    )
    return (
        output,
        grad_inputs,
        shard_ln1_gain,
        shard_ln1_bias,
        shard_w_query,
        shard_b_query,
        shard_w_key,
        shard_w_value,
        shard_b_value,
        shard_w_out,
        shard_b_out,
        shard_ln2_gain,
        shard_ln2_bias,
        shard_w_up,
        shard_b_up,
        shard_w_down,
        shard_b_down,
    )


def solution(mesh):
    in_specs = (
        P("fsdp", None),
        P("fsdp"),
        P("fsdp"),
        P("fsdp", None),
        P("fsdp"),
        P("fsdp", None),
        P("fsdp", None),
        P("fsdp"),
        P("fsdp", None),
        P("fsdp"),
        P("fsdp"),
        P("fsdp"),
        P("fsdp", None),
        P("fsdp"),
        P("fsdp", None),
        P("fsdp"),
        P(),
        P("fsdp", None),
    )
    out_specs = (
        P("fsdp", None),
        P("fsdp", None),
        P("fsdp"),
        P("fsdp"),
        P("fsdp", None),
        P("fsdp"),
        P("fsdp", None),
        P("fsdp", None),
        P("fsdp"),
        P("fsdp", None),
        P("fsdp"),
        P("fsdp"),
        P("fsdp"),
        P("fsdp", None),
        P("fsdp"),
        P("fsdp", None),
        P("fsdp"),
    )
    return jax.shard_map(
        on_device, mesh=mesh, in_specs=in_specs, out_specs=out_specs, check_vma=False
    )
```

profile of v0, /device:TPU:14, one launch (start us, length us, event | category | flops | bytes accessed | tf_op | source)
XLA Modules:
  0.0 1651.8 jit_solution(5950444463934327169)
XLA Ops:
  20.4 42.8 %all-reduce.19 = (bf16[1280]{0:T(1024)(128)(2,1)S(1)}, bf16[1280]{0:T(1024)(128)(2,1)S(1)}, bf16[1280]{0:T(1024)(128)(2,1)S(1)}, bf16[1280]{0:T(1024)(128)(2,1)S...) all-reduce(bf16[1280]{0:T(1024)(128)(2,1)S(1)} %dynamic-update-slic, ...), channel_id=1, replica_groups=mesh['fsdp'=32] {'fsdp'}, use_global_device_ids=true, to_apply=%add.2 | all-reduce | flops 15360 | bytes 61440
  63.6 7.3 all-gather.9.cloned.1.call-done
  74.0 58.3 %all-gather.11.cloned.1.call-done = bf16[1280,1280]{1,0:T(8,128)(2,1)} async-done(((bf16[40,1280]{1,0:T(8,128)(2,1)}), bf16[1280,1280]{1,0:T(8,128)(2,1)}) %all-gather.11.cloned.1.call-update) | async-done | bytes 3276816 | tf_op jit(solution)/shard_map/all_gather | solution.py:116
  139.6 22.7 %collective-permute-done.1 = bf16[384,1280]{1,0:T(8,128)(2,1)S(1)} collective-permute-done((bf16[384,1280]{1,0:T(8,128)(2,1)}, bf16[384,1280]{1,0:T(8,128)(2,1)S(1)}, u32[]{:S(2)}, u32[]{:S(2)}) %collective-permute-start.1) | collective-permute-done | bytes 983072 | tf_op jit(solution)/shard_map/ppermute | solution.py:22
  167.7 22.0 %collective-permute-done.4 = bf16[384,1280]{1,0:T(8,128)(2,1)S(1)} collective-permute-done((bf16[384,1280]{1,0:T(8,128)(2,1)S(1)}, bf16[384,1280]{1,0:T(8,128)(2,1)S(1)}, u32[]{:S(2)}, u32[]{:S(2)}) %collective-permute-start.4) | collective-permute-done | bytes 983072 | tf_op jit(solution)/shard_map/ppermute | solution.py:22
  233.8 7.7 copy.138
  241.5 24.0 %collective-permute-done.5 = bf16[768,1280]{1,0:T(8,128)(2,1)} collective-permute-done((bf16[768,1280]{1,0:T(8,128)(2,1)}, bf16[768,1280]{1,0:T(8,128)(2,1)}, u32[]{:S(2)}, u32[]{:S(2)}) %collective-permute-start.5) | collective-permute-done | bytes 1966112 | tf_op jit(solution)/shard_map/ppermute | solution.py:22
  274.3 7.8 copy.139
  282.2 84.0 %while.28 = (s32[]{:T(128)}, bf16[16,192,80]{1,2,0:T(8,128)(2,1)S(1)}, f32[16,192]{1,0:T(8,128)}, bf16[16,192,80]{2,1,0:T(8,128)(2,1)}, bf16[16,1536,80]{2,1,0:T...) while((s32[]{:T(128)}, ...), condition=%wide.region_5.6_spmd.clone, body=%wide.region_2.5_spmd.clone.sunk | while | flops 96732480 | bytes 4469869 | solution.py:176
  369.4 9.5 convolution_add_fusion
  378.8 87.4 %all-gather.17.cloned.1.call-done = bf16[5120,1280]{1,0:T(8,128)(2,1)} async-done(((bf16[160,1280]{1,0:T(8,128)(2,1)}), bf16[5120,1280]{1,0:T(8,128)(2,1)}) %all-gather.17.cloned.1.call-update) | async-done | bytes 13107216 | tf_op jit(solution)/shard_map/all_gather | solution.py:124
  466.2 17.2 %convert_reduce_fusion = (f32[5120]{0:T(1024)S(1)}, bf16[192,5120]{1,0:T(8,128)(2,1)S(1)}, f32[192,5120]{1,0:T(8,128)}) fusion(f32[192,5120]{1,0:T(8,128)} %convolution_add_fusion, bf16[192,1280]{1,0:T(8,128)(2,1)S(1)} %copy-done.7, bf16[5120,1280]{1,0:T(8,128)(2,1)} %all-gather.17.cloned.1.call-done), kind=kOutput, calls=%fused_computation.70 | convolution fusion | flops 2589322240 | bytes 23449600 | tf_op jit(solution)/shard_map/dot_general | solution.py:57
  483.4 10.1 multiply_reduce_fusion.1
  498.2 153.4 %while.29 = (s32[]{:T(128)}, bf16[16,192,80]{1,2,0:T(8,128)(2,1)S(1)}, f32[16,1536,80]{1,2,0:T(8,128)}, f32[16,1536,80]{1,2,0:T(8,128)}, bf16[16,192,80]{2,1,0:T...) while((s32[]{:T(128)}, ...), condition=%wide.region_12.13_spmd.clone, body=%wide.region_10.12_spmd.clone.sunk | while | flops 238723392 | bytes 11284349 | solution.py:233
  688.6 5.9 copy.148
  698.5 8.2 collective-permute-done.6
  710.7 37.5 %collective-permute-done.9 = bf16[768,1280]{1,0:T(8,128)(2,1)} collective-permute-done((bf16[768,1280]{1,0:T(8,128)(2,1)}, bf16[768,1280]{1,0:T(8,128)(2,1)}, u32[]{:S(2)}, u32[]{:S(2)}) %collective-permute-start.9) | collective-permute-done | bytes 1966112 | tf_op jit(solution)/shard_map/ppermute | solution.py:22
  752.4 21.1 %collective-permute-done.10 = bf16[384,1280]{1,0:T(8,128)(2,1)S(1)} collective-permute-done((bf16[384,1280]{1,0:T(8,128)(2,1)S(1)}, bf16[384,1280]{1,0:T(8,128)(2,1)S(1)}, u32[]{:S(2)}, u32[]{:S(2)}) %collective-permute-start.10) | collective-permute-done | bytes 983072 | tf_op jit(solution)/shard_map/ppermute | solution.py:22
  786.3 10.7 convolution_dynamic-update-slice_fusion
  801.0 11.2 fusion.87
  817.8 8.6 fusion.55
  831.9 47.0 %all-reduce.18 = (f32[1280]{0:T(1024)S(1)}, f32[1280]{0:T(1024)S(1)}, f32[1280]{0:T(1024)S(1)}, f32[1280]{0:T(1024)S(1)}, f32[1280]{0:T(1024)S(1)}, /*index=5*/f...) all-reduce(f32[1280]{0:T(1024)S(1)} %get-tuple-element.224, ...), channel_id=2, replica_groups=mesh['fsdp'=32] {'fsdp'}, use_global_device_ids=true, to_apply=%region_16.17.clone | all-reduce | flops 15360 | bytes 122880
  884.3 472.3 %reduce-scatter.3.cloned.1.call-done = f32[40,10240]{1,0:T(8,128)} async-done(((f32[1280,10240]{1,0:T(8,128)}), f32[40,10240]{1,0:T(8,128)}) %reduce-scatter.3.cloned.1.call-update) | async-done | bytes 1638416 | tf_op jit(solution)/shard_map/reduce_scatter | solution.py:267
  1360.8 284.0 %reduce-scatter.5.cloned.1.call-done = f32[160,1280]{1,0:T(8,128)} async-done(((f32[5120,1280]{1,0:T(8,128)}), f32[160,1280]{1,0:T(8,128)}) %reduce-scatter.5.cloned.1.call-update) | async-done | bytes 819216 | tf_op jit(solution)/shard_map/reduce_scatter | solution.py:208
  (461 shorter events, 412.7 us)
Async XLA Ops:
  7.3 55.9 %copy-start = (bf16[192,1280]{1,0:T(8,128)(2,1)S(1)}, bf16[192,1280]{1,0:T(8,128)(2,1)}, u32[]{:S(2)}) copy-start(bf16[192,1280]{1,0:T(8,128)(2,1)} %param.22) | copy-start | bytes 1474564
  7.3 63.6 %all-gather.9.cloned.1.call-start = ((), (), s32[]{:S(2)}) async-start(), calls=%async_computation.3 | async-start | bytes 3379200 | tf_op jit(solution)/shard_map/all_gather | solution.py:115
  9.0 123.3 %all-gather.11.cloned.1.call-start = ((), (), s32[]{:S(2)}) async-start(), calls=%async_computation.4 | async-start | bytes 3379200 | tf_op jit(solution)/shard_map/all_gather | solution.py:116
  10.7 191.3 %all-gather.7.cloned.1.call-start = ((), (), s32[]{:S(2)}) async-start(), calls=%async_computation.2 | async-start | bytes 3379200 | tf_op jit(solution)/shard_map/all_gather | solution.py:113
  12.3 353.8 %all-gather.13.cloned.1.call-start = ((), (), s32[]{:S(2)}) async-start(), calls=%async_computation.5 | async-start | bytes 3379200 | tf_op jit(solution)/shard_map/all_gather | solution.py:118
  14.0 355.3 %all-gather.15.cloned.1.call-start = ((), (), s32[]{:S(2)}) async-start(), calls=%async_computation.6 | async-start | bytes 13516800 | tf_op jit(solution)/shard_map/all_gather | solution.py:122
  16.0 450.1 %all-gather.17.cloned.1.call-start = ((), (), s32[]{:S(2)}) async-start(), calls=%async_computation.7 | async-start | bytes 13516800 | tf_op jit(solution)/shard_map/all_gather | solution.py:124
  18.1 1338.5 %reduce-scatter.3.cloned.1.call-start = ((), (), s32[]{:S(2)}) async-start(), calls=%async_computation.8 | async-start | bytes 54067200 | tf_op jit(solution)/shard_map/reduce_scatter | solution.py:267
  63.6 71.6 %copy-start.24 = (f32[192]{0:T(256)}, f32[192]{0:T(256)S(1)}, u32[]{:S(2)}) copy-start(f32[192]{0:T(256)S(1)} %fusion.67) | copy-start | bytes 2308
  73.7 64.5 %copy-start.21 = (bf16[192,1280]{1,0:T(8,128)(2,1)}, bf16[192,1280]{1,0:T(8,128)(2,1)S(1)}, u32[]{:S(2)}) copy-start(bf16[192,1280]{1,0:T(8,128)(2,1)S(1)} %convolution_convert_fusion.1) | copy-start | bytes 1474564
  73.7 61.8 %collective-permute-start = (bf16[192,1280]{1,0:T(8,128)(2,1)S(1)}, bf16[192,1280]{1,0:T(8,128)(2,1)S(1)}, u32[]{:S(2)}, u32[]{:S(2)}) collective-permute-start(bf16[192,1280]{1,0:T(8,128)(2,1)S(1)} %convolution_convert_fusion.1), channel_id=1, source_target_pairs={{0,1},{1,0},{2,3},{3,2},{4,5},{5,4},{6,7},{7,6},{8,9},{9,8},{10,11... | collective-permute-start | bytes 1474568 | tf_op jit(solution)/shard_map/ppermute | solution.py:22
  135.2 3.0 collective-permute-start.3
  136.7 25.6 %collective-permute-start.1 = (bf16[384,1280]{1,0:T(8,128)(2,1)}, bf16[384,1280]{1,0:T(8,128)(2,1)S(1)}, u32[]{:S(2)}, u32[]{:S(2)}) collective-permute-start(bf16[384,1280]{1,0:T(8,128)(2,1)} %maximum_select_fusion.6), channel_id=1, source_target_pairs={{0,2},{2,0},{1,3},{3,1},{4,6},{6,4},{5,7},{7,5},{8,10},{10,8},{9,1... | collective-permute-start | bytes 2949128 | tf_op jit(solution)/shard_map/ppermute | solution.py:22
  139.0 50.6 %collective-permute-start.4 = (bf16[384,1280]{1,0:T(8,128)(2,1)S(1)}, bf16[384,1280]{1,0:T(8,128)(2,1)S(1)}, u32[]{:S(2)}, u32[]{:S(2)}) collective-permute-start(bf16[384,1280]{1,0:T(8,128)(2,1)S(1)} %maximum_select_fusion.8), channel_id=1, source_target_pairs={{0,2},{2,0},{1,3},{3,1},{4,6},{6,4},{5,7},{7,5},{8,10},{10,8},{9,1... | collective-permute-start | bytes 2949128 | tf_op jit(solution)/shard_map/ppermute | solution.py:22
  165.9 58.2 %collective-permute-start.2 = (bf16[768,1280]{1,0:T(8,128)(2,1)}, bf16[768,1280]{1,0:T(8,128)(2,1)}, u32[]{:S(2)}, u32[]{:S(2)}) collective-permute-start(bf16[768,1280]{1,0:T(8,128)(2,1)} %maximum_select_fusion.2), channel_id=1, source_target_pairs={{0,4},{4,0},{1,5},{5,1},{2,6},{6,2},{3,7},{7,3},{8,12},{12,8},{9,1... | collective-permute-start | bytes 5898248 | tf_op jit(solution)/shard_map/ppermute | solution.py:22
  191.7 73.9 %collective-permute-start.5 = (bf16[768,1280]{1,0:T(8,128)(2,1)}, bf16[768,1280]{1,0:T(8,128)(2,1)}, u32[]{:S(2)}, u32[]{:S(2)}) collective-permute-start(bf16[768,1280]{1,0:T(8,128)(2,1)} %maximum_select_fusion.4), channel_id=1, source_target_pairs={{0,4},{4,0},{1,5},{5,1},{2,6},{6,2},{3,7},{7,3},{8,12},{12,8},{9,1... | collective-permute-start | bytes 5898248 | tf_op jit(solution)/shard_map/ppermute | solution.py:22
  369.3 96.9 %copy-start.7 = (bf16[192,1280]{1,0:T(8,128)(2,1)S(1)}, bf16[192,1280]{1,0:T(8,128)(2,1)}, u32[]{:S(2)}) copy-start(bf16[192,1280]{1,0:T(8,128)(2,1)} %param.39) | copy-start | bytes 1474564
  660.7 46.0 %collective-permute-start.6 = (bf16[768,1280]{1,0:T(8,128)(2,1)}, bf16[768,1280]{1,0:T(8,128)(2,1)}, u32[]{:S(2)}, u32[]{:S(2)}) collective-permute-start(bf16[768,1280]{1,0:T(8,128)(2,1)} %copy.145), channel_id=1, source_target_pairs={{0,4},{4,0},{1,5},{5,1},{2,6},{6,2},{3,7},{7,3},{8,12},{12,8},{9,1... | collective-permute-start | bytes 5898248 | tf_op jit(solution)/shard_map/ppermute | solution.py:22
  671.0 77.1 %collective-permute-start.9 = (bf16[768,1280]{1,0:T(8,128)(2,1)}, bf16[768,1280]{1,0:T(8,128)(2,1)}, u32[]{:S(2)}, u32[]{:S(2)}) collective-permute-start(bf16[768,1280]{1,0:T(8,128)(2,1)} %copy.147), channel_id=1, source_target_pairs={{0,4},{4,0},{1,5},{5,1},{2,6},{6,2},{3,7},{7,3},{8,12},{12,8},{9,1... | collective-permute-start | bytes 5898248 | tf_op jit(solution)/shard_map/ppermute | solution.py:22
  709.1 42.8 %collective-permute-start.7 = (bf16[384,1280]{1,0:T(8,128)(2,1)S(1)}, bf16[384,1280]{1,0:T(8,128)(2,1)S(1)}, u32[]{:S(2)}, u32[]{:S(2)}) collective-permute-start(bf16[384,1280]{1,0:T(8,128)(2,1)S(1)} %select_convert_fusion.3), channel_id=1, source_target_pairs={{0,2},{2,0},{1,3},{3,1},{4,6},{6,4},{5,7},{7,5},{8,10},{10,8},{9,1... | collective-permute-start | bytes 2949128 | tf_op jit(solution)/shard_map/ppermute | solution.py:22
  750.4 23.1 %collective-permute-start.10 = (bf16[384,1280]{1,0:T(8,128)(2,1)S(1)}, bf16[384,1280]{1,0:T(8,128)(2,1)S(1)}, u32[]{:S(2)}, u32[]{:S(2)}) collective-permute-start(bf16[384,1280]{1,0:T(8,128)(2,1)S(1)} %select_convert_fusion.2), channel_id=1, source_target_pairs={{0,2},{2,0},{1,3},{3,1},{4,6},{6,4},{5,7},{7,5},{8,10},{10,8},{9,1... | collective-permute-start | bytes 2949128 | tf_op jit(solution)/shard_map/ppermute | solution.py:22
  752.3 21.8 %collective-permute-start.8 = (bf16[192,1280]{1,0:T(8,128)(2,1)S(1)}, bf16[192,1280]{1,0:T(8,128)(2,1)S(1)}, u32[]{:S(2)}, u32[]{:S(2)}) collective-permute-start(bf16[192,1280]{1,0:T(8,128)(2,1)S(1)} %select_convert_fusion.5), channel_id=1, source_target_pairs={{0,1},{1,0},{2,3},{3,2},{4,5},{5,4},{6,7},{7,6},{8,9},{9,8},{10,11... | collective-permute-start | bytes 1474568 | tf_op jit(solution)/shard_map/ppermute | solution.py:22
  774.0 4.3 collective-permute-start.11
  797.1 847.7 %reduce-scatter.5.cloned.1.call-start = ((), (), s32[]{:S(2)}) async-start(), calls=%async_computation.9 | async-start | bytes 27033600 | tf_op jit(solution)/shard_map/reduce_scatter | solution.py:208
  (33 other events, 331.9 us)
Sparse Core Ops, SparseCore 0:
  11.5 59.2 all-gather.8
  74.3 57.9 all-gather.10
  135.8 66.1 all-gather.6
  205.3 63.3 all-gather.12
  271.4 95.7 all-gather.14
  369.9 96.2 all-gather.16
  797.2 559.3 reduce-scatter.2
  1359.4 285.2 reduce-scatter.4
where the time goes:
time: 1660 us; the launch traced here: 1650 us
  waiting for transfers between devices  1050 us (63%)
  matrix products  277 us (17%)
  local copies, waits for them, and re-layouts  107 us (6%)
  other arithmetic  102 us (6%)
  blocking collectives  89.8 us (5%)
    reduce_scatter x1, waiting for transfers between devices, on_device(): lax.psum_scatter(jnp.concatenate([jnp.concatenate([outer_sum(normed, grad...  472 us
    reduce_scatter x1, waiting for transfers between devices, on_device(): lax.psum_scatter(outer_sum(activated, cotangent), 'fsdp', scatter_dimensi...  284 us
    ppermute x12, waiting for transfers between devices, swapped(): return lax.ppermute(block, axis, route)  136 us
    dot_general x54, matrix products, times_transposed(): lax.dot_general(left, right, (((1,), (1,)), ((), ())), preferred_element_...  106 us
    dot_general x38, matrix products, outer_sum(): lax.dot_general(left, right, (((0,), (0,)), ((), ())), preferred_element_...  96.5 us
    unnamed x2, blocking collectives  89.8 us
    all_gather x1, waiting for transfers between devices, on_device(): lax.all_gather(w_down.astype(jnp.bfloat16), 'fsdp', axis=0, tiled=True)  87.4 us
    dot_general x38, matrix products, matmul(): return jnp.dot(left, right, preferred_element_type=jnp.float32)  74.9 us
  transfers between devices with their start and end apart: 20, of which 12 were waited for; matrix products, arithmetic and copies ran while one was open for 16% of the time, Pallas kernels for 0%

commit v1 on v0

--- a/solution.py
+++ b/solution.py
@@ -91,6 +91,13 @@
     lengths,
     cotangent,
 ):
+
+    def samples_cover(local_x, link_axis):
+        met_up = lax.axis_size(link_axis)
+        t1 = jnp.stack([local_x] * met_up)
+        upper = lax.all_to_all(t1, axis_name=link_axis, split_axis=0, concat_axis=0)
+        return jnp.concatenate(upper, axis=0)
+
     (
         whole_ln1_gain,
         whole_ln1_bias,
@@ -121,7 +128,7 @@
         lax.all_gather(ln2_bias.astype(jnp.bfloat16), "fsdp", axis=0, tiled=True),
         lax.all_gather(w_up.astype(jnp.bfloat16), "fsdp", axis=0, tiled=True),
         lax.all_gather(b_up.astype(jnp.bfloat16), "fsdp", axis=0, tiled=True),
-        lax.all_gather(w_down.astype(jnp.bfloat16), "fsdp", axis=0, tiled=True),
+        samples_cover(w_down.astype(jnp.bfloat16), "fsdp"),
         lax.all_gather(b_down.astype(jnp.bfloat16), "fsdp", axis=0, tiled=True),
     )
     device_index = lax.axis_index("fsdp")

time: 1660 us -> 1850 us (1.11)
  waiting for transfers between devices: 1050 us -> 1150 us
  blocking collectives: 89.8 us -> 161 us
    all_to_all x0 -> x1, waiting for transfers between devices: none -> 341 us  [samples_cover(): upper = lax.all_to_all(t1, axis_name=link_axis, split_axis=0, concat_axis=0)]
    reduce_scatter x1, waiting for transfers between devices: 472 us -> 217 us  [on_device(): lax.psum_scatter(jnp.concatenate([jnp.concatenate([outer_sum(normed, grad...]
    unnamed x2, blocking collectives: 89.8 us -> 161 us
  transfers between devices with their start and end apart: 20 -> 21, of which waited for: 12 -> 13; matrix products, arithmetic and copies ran while one was open for 16% -> 15% of each run, Pallas kernels for 0% -> 0%
where the time goes in v1:
time: 1850 us; the launch traced here: 1840 us
  waiting for transfers between devices  1150 us (62%)
  matrix products  278 us (15%)
  blocking collectives  161 us (9%)
  local copies, waits for them, and re-layouts  113 us (6%)
  other arithmetic  101 us (5%)
    all_to_all x1, waiting for transfers between devices, samples_cover(): upper = lax.all_to_all(t1, axis_name=link_axis, split_axis=0, concat_axis=0)  341 us
    reduce_scatter x1, waiting for transfers between devices, on_device(): lax.psum_scatter(outer_sum(activated, cotangent), 'fsdp', scatter_dimensi...  296 us
    reduce_scatter x1, waiting for transfers between devices, on_device(): lax.psum_scatter(jnp.concatenate([jnp.concatenate([outer_sum(normed, grad...  217 us
    unnamed x2, blocking collectives  161 us
    ppermute x12, waiting for transfers between devices, swapped(): return lax.ppermute(block, axis, route)  136 us
    dot_general x54, matrix products, times_transposed(): lax.dot_general(left, right, (((1,), (1,)), ((), ())), preferred_element_...  107 us
    dot_general x38, matrix products, outer_sum(): lax.dot_general(left, right, (((0,), (0,)), ((), ())), preferred_element_...  96.5 us
    all_gather x1, waiting for transfers between devices, on_device(): lax.all_gather(w_down.astype(jnp.bfloat16), 'fsdp', axis=0, tiled=True)  87.6 us
  transfers between devices with their start and end apart: 21, of which 13 were waited for; matrix products, arithmetic and copies ran while one was open for 15% of the time, Pallas kernels for 0%

profile of v1, /device:TPU:14, one launch (start us, length us, event | category | flops | bytes accessed | tf_op | source)
XLA Modules:
  0.0 1835.6 jit_solution(8402858360729319440)
XLA Ops:
  20.4 42.1 %all-reduce.19 = (bf16[1280]{0:T(1024)(128)(2,1)S(1)}, bf16[1280]{0:T(1024)(128)(2,1)S(1)}, bf16[1280]{0:T(1024)(128)(2,1)S(1)}, bf16[1280]{0:T(1024)(128)(2,1)S...) all-reduce(bf16[1280]{0:T(1024)(128)(2,1)S(1)} %dynamic-update-slic, ...), channel_id=1, replica_groups=mesh['fsdp'=32] {'fsdp'}, use_global_device_ids=true, to_apply=%add.2 | all-reduce | flops 15360 | bytes 61440
  63.0 7.7 all-gather.9.cloned.1.call-done
  73.8 58.2 %all-gather.11.cloned.1.call-done = bf16[1280,1280]{1,0:T(8,128)(2,1)} async-done(((bf16[40,1280]{1,0:T(8,128)(2,1)}), bf16[1280,1280]{1,0:T(8,128)(2,1)}) %all-gather.11.cloned.1.call-update) | async-done | bytes 3276816 | tf_op jit(solution)/shard_map/all_gather | solution.py:123
  139.2 22.8 %collective-permute-done.1 = bf16[384,1280]{1,0:T(8,128)(2,1)S(1)} collective-permute-done((bf16[384,1280]{1,0:T(8,128)(2,1)}, bf16[384,1280]{1,0:T(8,128)(2,1)S(1)}, u32[]{:S(2)}, u32[]{:S(2)}) %collective-permute-start.1) | collective-permute-done | bytes 983072 | tf_op jit(solution)/shard_map/ppermute | solution.py:22
  167.2 22.2 %collective-permute-done.4 = bf16[384,1280]{1,0:T(8,128)(2,1)S(1)} collective-permute-done((bf16[384,1280]{1,0:T(8,128)(2,1)S(1)}, bf16[384,1280]{1,0:T(8,128)(2,1)S(1)}, u32[]{:S(2)}, u32[]{:S(2)}) %collective-permute-start.4) | collective-permute-done | bytes 983072 | tf_op jit(solution)/shard_map/ppermute | solution.py:22
  233.3 7.7 copy.138
  241.0 24.2 %collective-permute-done.5 = bf16[768,1280]{1,0:T(8,128)(2,1)} collective-permute-done((bf16[768,1280]{1,0:T(8,128)(2,1)}, bf16[768,1280]{1,0:T(8,128)(2,1)}, u32[]{:S(2)}, u32[]{:S(2)}) %collective-permute-start.5) | collective-permute-done | bytes 1966112 | tf_op jit(solution)/shard_map/ppermute | solution.py:22
  273.9 7.8 copy.139
  281.8 84.0 %while.28 = (s32[]{:T(128)}, bf16[16,192,80]{1,2,0:T(8,128)(2,1)S(1)}, f32[16,192]{1,0:T(8,128)}, bf16[16,192,80]{2,1,0:T(8,128)(2,1)}, bf16[16,1536,80]{2,1,0:T...) while((s32[]{:T(128)}, ...), condition=%wide.region_5.6_spmd.clone, body=%wide.region_2.5_spmd.clone.sunk | while | flops 96732480 | bytes 4469869 | solution.py:183
  368.9 9.5 convolution_add_fusion
  378.4 87.6 %all-gather.17.cloned.1.call-done = bf16[5120,1280]{1,0:T(8,128)(2,1)} async-done(((bf16[160,1280]{1,0:T(8,128)(2,1)}), bf16[5120,1280]{1,0:T(8,128)(2,1)}) %all-gather.17.cloned.1.call-update) | async-done | bytes 13107216 | tf_op jit(solution)/shard_map/all_gather | solution.py:207
  466.0 17.3 convert_reduce_fusion
  483.3 10.1 multiply_reduce_fusion.1
  498.1 153.3 %while.29 = (s32[]{:T(128)}, bf16[16,192,80]{1,2,0:T(8,128)(2,1)S(1)}, f32[16,1536,80]{1,2,0:T(8,128)}, f32[16,1536,80]{1,2,0:T(8,128)}, bf16[16,192,80]{2,1,0:T...) while((s32[]{:T(128)}, ...), condition=%wide.region_12.13_spmd.clone, body=%wide.region_10.12_spmd.clone.sunk | while | flops 238723392 | bytes 11284349 | solution.py:240
  698.1 8.5 collective-permute-done.6
  710.5 37.5 %collective-permute-done.9 = bf16[768,1280]{1,0:T(8,128)(2,1)} collective-permute-done((bf16[768,1280]{1,0:T(8,128)(2,1)}, bf16[768,1280]{1,0:T(8,128)(2,1)}, u32[]{:S(2)}, u32[]{:S(2)}) %collective-permute-start.9) | collective-permute-done | bytes 1966112 | tf_op jit(solution)/shard_map/ppermute | solution.py:22
  752.3 21.1 %collective-permute-done.10 = bf16[384,1280]{1,0:T(8,128)(2,1)S(1)} collective-permute-done((bf16[384,1280]{1,0:T(8,128)(2,1)S(1)}, bf16[384,1280]{1,0:T(8,128)(2,1)S(1)}, u32[]{:S(2)}, u32[]{:S(2)}) %collective-permute-start.10) | collective-permute-done | bytes 983072 | tf_op jit(solution)/shard_map/ppermute | solution.py:22
  786.2 10.7 convolution_dynamic-update-slice_fusion
  800.9 11.2 fusion.87
  830.8 341.4 %all-to-all-done = bf16[32,160,1280]{2,1,0:T(8,128)(2,1)} async-done(((bf16[32,160,1280]{2,1,0:T(8,128)(2,1)}), bf16[32,160,1280]{2,1,0:T(8,128)(2,1)}, u32[]{:S(2)}, u32[]{:S(2)}) %all-to-all-start) | async-done | bytes 13107232 | tf_op jit(solution)/shard_map/all_to_all | solution.py:98
  1172.1 8.7 fusion.55
  1186.3 119.4 %all-reduce.18 = (f32[1280]{0:T(1024)S(1)}, f32[1280]{0:T(1024)S(1)}, f32[1280]{0:T(1024)S(1)}, f32[1280]{0:T(1024)S(1)}, f32[1280]{0:T(1024)S(1)}, /*index=5*/f...) all-reduce(f32[1280]{0:T(1024)S(1)} %get-tuple-element.224, ...), channel_id=2, replica_groups=mesh['fsdp'=32] {'fsdp'}, use_global_device_ids=true, to_apply=%region_16.17.clone | all-reduce | flops 15360 | bytes 122880
  1311.0 217.4 %reduce-scatter.3.cloned.1.call-done = f32[40,10240]{1,0:T(8,128)} async-done(((f32[1280,10240]{1,0:T(8,128)}), f32[40,10240]{1,0:T(8,128)}) %reduce-scatter.3.cloned.1.call-update) | async-done | bytes 1638416 | tf_op jit(solution)/shard_map/reduce_scatter | solution.py:274
  1532.6 296.0 %reduce-scatter.5.cloned.1.call-done = f32[160,1280]{1,0:T(8,128)} async-done(((f32[5120,1280]{1,0:T(8,128)}), f32[160,1280]{1,0:T(8,128)}) %reduce-scatter.5.cloned.1.call-update) | async-done | bytes 819216 | tf_op jit(solution)/shard_map/reduce_scatter | solution.py:215
  (466 shorter events, 431.0 us)
Async XLA Ops:
  7.3 63.4 %all-gather.9.cloned.1.call-start = ((), (), s32[]{:S(2)}) async-start(), calls=%async_computation.4 | async-start | bytes 3379200 | tf_op jit(solution)/shard_map/all_gather | solution.py:122
  9.0 123.0 %all-gather.11.cloned.1.call-start = ((), (), s32[]{:S(2)}) async-start(), calls=%async_computation.5 | async-start | bytes 3379200 | tf_op jit(solution)/shard_map/all_gather | solution.py:123
  10.7 191.0 %all-gather.7.cloned.1.call-start = ((), (), s32[]{:S(2)}) async-start(), calls=%async_computation.3 | async-start | bytes 3379200 | tf_op jit(solution)/shard_map/all_gather | solution.py:120
  12.3 353.4 %all-gather.13.cloned.1.call-start = ((), (), s32[]{:S(2)}) async-start(), calls=%async_computation.6 | async-start | bytes 3379200 | tf_op jit(solution)/shard_map/all_gather | solution.py:125
  14.0 354.9 %all-gather.15.cloned.1.call-start = ((), (), s32[]{:S(2)}) async-start(), calls=%async_computation.7 | async-start | bytes 13516800 | tf_op jit(solution)/shard_map/all_gather | solution.py:129
  16.1 450.0 %all-gather.17.cloned.1.call-start = ((), (), s32[]{:S(2)}) async-start(), calls=%async_computation.8 | async-start | bytes 13516800 | tf_op jit(solution)/shard_map/all_gather | solution.py:207
  18.1 1510.3 %reduce-scatter.3.cloned.1.call-start = ((), (), s32[]{:S(2)}) async-start(), calls=%async_computation.9 | async-start | bytes 54067200 | tf_op jit(solution)/shard_map/reduce_scatter | solution.py:274
  63.0 71.8 %copy-start.25 = (f32[192]{0:T(256)}, f32[192]{0:T(256)S(1)}, u32[]{:S(2)}) copy-start(f32[192]{0:T(256)S(1)} %fusion.67) | copy-start | bytes 2308
  73.5 64.4 %copy-start.21 = (bf16[192,1280]{1,0:T(8,128)(2,1)}, bf16[192,1280]{1,0:T(8,128)(2,1)S(1)}, u32[]{:S(2)}) copy-start(bf16[192,1280]{1,0:T(8,128)(2,1)S(1)} %convolution_convert_fusion.1) | copy-start | bytes 1474564
  73.5 61.6 %collective-permute-start = (bf16[192,1280]{1,0:T(8,128)(2,1)S(1)}, bf16[192,1280]{1,0:T(8,128)(2,1)S(1)}, u32[]{:S(2)}, u32[]{:S(2)}) collective-permute-start(bf16[192,1280]{1,0:T(8,128)(2,1)S(1)} %convolution_convert_fusion.1), channel_id=1, source_target_pairs={{0,1},{1,0},{2,3},{3,2},{4,5},{5,4},{6,7},{7,6},{8,9},{9,8},{10,11... | collective-permute-start | bytes 1474568 | tf_op jit(solution)/shard_map/ppermute | solution.py:22
  134.8 3.0 collective-permute-start.3
  136.4 25.6 %collective-permute-start.1 = (bf16[384,1280]{1,0:T(8,128)(2,1)}, bf16[384,1280]{1,0:T(8,128)(2,1)S(1)}, u32[]{:S(2)}, u32[]{:S(2)}) collective-permute-start(bf16[384,1280]{1,0:T(8,128)(2,1)} %maximum_select_fusion.6), channel_id=1, source_target_pairs={{0,2},{2,0},{1,3},{3,1},{4,6},{6,4},{5,7},{7,5},{8,10},{10,8},{9,1... | collective-permute-start | bytes 2949128 | tf_op jit(solution)/shard_map/ppermute | solution.py:22
  138.7 50.7 %collective-permute-start.4 = (bf16[384,1280]{1,0:T(8,128)(2,1)S(1)}, bf16[384,1280]{1,0:T(8,128)(2,1)S(1)}, u32[]{:S(2)}, u32[]{:S(2)}) collective-permute-start(bf16[384,1280]{1,0:T(8,128)(2,1)S(1)} %maximum_select_fusion.8), channel_id=1, source_target_pairs={{0,2},{2,0},{1,3},{3,1},{4,6},{6,4},{5,7},{7,5},{8,10},{10,8},{9,1... | collective-permute-start | bytes 2949128 | tf_op jit(solution)/shard_map/ppermute | solution.py:22
  165.4 58.1 %collective-permute-start.2 = (bf16[768,1280]{1,0:T(8,128)(2,1)}, bf16[768,1280]{1,0:T(8,128)(2,1)}, u32[]{:S(2)}, u32[]{:S(2)}) collective-permute-start(bf16[768,1280]{1,0:T(8,128)(2,1)} %maximum_select_fusion.2), channel_id=1, source_target_pairs={{0,4},{4,0},{1,5},{5,1},{2,6},{6,2},{3,7},{7,3},{8,12},{12,8},{9,1... | collective-permute-start | bytes 5898248 | tf_op jit(solution)/shard_map/ppermute | solution.py:22
  191.3 73.8 %collective-permute-start.5 = (bf16[768,1280]{1,0:T(8,128)(2,1)}, bf16[768,1280]{1,0:T(8,128)(2,1)}, u32[]{:S(2)}, u32[]{:S(2)}) collective-permute-start(bf16[768,1280]{1,0:T(8,128)(2,1)} %maximum_select_fusion.4), channel_id=1, source_target_pairs={{0,4},{4,0},{1,5},{5,1},{2,6},{6,2},{3,7},{7,3},{8,12},{12,8},{9,1... | collective-permute-start | bytes 5898248 | tf_op jit(solution)/shard_map/ppermute | solution.py:22
  368.9 97.1 %copy-start.7 = (bf16[192,1280]{1,0:T(8,128)(2,1)S(1)}, bf16[192,1280]{1,0:T(8,128)(2,1)}, u32[]{:S(2)}) copy-start(bf16[192,1280]{1,0:T(8,128)(2,1)} %param.39) | copy-start | bytes 1474564
  660.6 46.0 %collective-permute-start.6 = (bf16[768,1280]{1,0:T(8,128)(2,1)}, bf16[768,1280]{1,0:T(8,128)(2,1)}, u32[]{:S(2)}, u32[]{:S(2)}) collective-permute-start(bf16[768,1280]{1,0:T(8,128)(2,1)} %copy.145), channel_id=1, source_target_pairs={{0,4},{4,0},{1,5},{5,1},{2,6},{6,2},{3,7},{7,3},{8,12},{12,8},{9,1... | collective-permute-start | bytes 5898248 | tf_op jit(solution)/shard_map/ppermute | solution.py:22
  671.0 77.0 %collective-permute-start.9 = (bf16[768,1280]{1,0:T(8,128)(2,1)}, bf16[768,1280]{1,0:T(8,128)(2,1)}, u32[]{:S(2)}, u32[]{:S(2)}) collective-permute-start(bf16[768,1280]{1,0:T(8,128)(2,1)} %copy.147), channel_id=1, source_target_pairs={{0,4},{4,0},{1,5},{5,1},{2,6},{6,2},{3,7},{7,3},{8,12},{12,8},{9,1... | collective-permute-start | bytes 5898248 | tf_op jit(solution)/shard_map/ppermute | solution.py:22
  709.0 42.8 %collective-permute-start.7 = (bf16[384,1280]{1,0:T(8,128)(2,1)S(1)}, bf16[384,1280]{1,0:T(8,128)(2,1)S(1)}, u32[]{:S(2)}, u32[]{:S(2)}) collective-permute-start(bf16[384,1280]{1,0:T(8,128)(2,1)S(1)} %select_convert_fusion.3), channel_id=1, source_target_pairs={{0,2},{2,0},{1,3},{3,1},{4,6},{6,4},{5,7},{7,5},{8,10},{10,8},{9,1... | collective-permute-start | bytes 2949128 | tf_op jit(solution)/shard_map/ppermute | solution.py:22
  750.3 23.1 %collective-permute-start.10 = (bf16[384,1280]{1,0:T(8,128)(2,1)S(1)}, bf16[384,1280]{1,0:T(8,128)(2,1)S(1)}, u32[]{:S(2)}, u32[]{:S(2)}) collective-permute-start(bf16[384,1280]{1,0:T(8,128)(2,1)S(1)} %select_convert_fusion.2), channel_id=1, source_target_pairs={{0,2},{2,0},{1,3},{3,1},{4,6},{6,4},{5,7},{7,5},{8,10},{10,8},{9,1... | collective-permute-start | bytes 2949128 | tf_op jit(solution)/shard_map/ppermute | solution.py:22
  752.2 21.8 %collective-permute-start.8 = (bf16[192,1280]{1,0:T(8,128)(2,1)S(1)}, bf16[192,1280]{1,0:T(8,128)(2,1)S(1)}, u32[]{:S(2)}, u32[]{:S(2)}) collective-permute-start(bf16[192,1280]{1,0:T(8,128)(2,1)S(1)} %select_convert_fusion.5), channel_id=1, source_target_pairs={{0,1},{1,0},{2,3},{3,2},{4,5},{5,4},{6,7},{7,6},{8,9},{9,8},{10,11... | collective-permute-start | bytes 1474568 | tf_op jit(solution)/shard_map/ppermute | solution.py:22
  773.9 4.4 collective-permute-start.11
  796.9 1031.7 %reduce-scatter.5.cloned.1.call-start = ((), (), s32[]{:S(2)}) async-start(), calls=%async_computation.10 | async-start | bytes 27033600 | tf_op jit(solution)/shard_map/reduce_scatter | solution.py:215
  819.2 352.9 %all-to-all-start = ((bf16[32,160,1280]{2,1,0:T(8,128)(2,1)}), bf16[32,160,1280]{2,1,0:T(8,128)(2,1)}, u32[]{:S(2)}, u32[]{:S(2)}) async-start(bf16[32,160,1280]{2,1,0:T(8,128)(2,1)} %stack.2), calls=%async_computation | async-start | bytes 26214400 | tf_op jit(solution)/shard_map/all_to_all | solution.py:98
  (35 other events, 401.1 us)
Sparse Core Ops, SparseCore 0:
  11.5 59.1 all-gather.8
  74.1 57.8 all-gather.10
  135.4 66.1 all-gather.6
  204.9 63.4 all-gather.12
  271.1 95.7 all-gather.14
  369.6 96.3 all-gather.16
  797.0 731.3 reduce-scatter.2
  1531.3 297.2 reduce-scatter.4
